TPU v7x, 32 devices: a whole 2x2x4 slice. The times are simulated.
32 devices in a mesh: row: 8 (over y, x, core), col: 4 (over z).
Axes of the slice: x: 2, y: 2, z: 4, core: 2. Of those that a mesh axis runs over, the one named last changes fastest.
Arguments:
- sub_basis: bfloat16 [32, 768, 768], P(('row', 'col')), may hold values from -0.15625 to 0.15625
- coupling: bfloat16 [32, 2, 768, 768], P(('row', 'col')), may hold values from -0.15625 to 0.15625
- pair_live: int32 [32, 2], P(('row', 'col')), may hold values 0 or 1
- offsets: int32 [32], P(('row', 'col')), may hold values from 0 to 3328
- dual_in: float32 [4, 4096], P('col', 'row'), may hold values from -6 to 6
Outputs:
- dual_out: float32 [4, 4096], P('col', 'row')
Inputs may be any that keep to these rules, and one draw needn't show every extreme that they name: `offsets`: each subdomain's window of 768 multipliers lies inside its block column's vector.
All inputs are finite; a program needn't handle non-finite values. No bound on the sum of `pair_live` on one device may be relied on, other than what follows from the above.
Results may differ from a plain program's by a relative error of at most 0.0085.
Values may be sent and summed in bfloat16 or wider, within the bound.
A program may use at most 64 MiB of HBM per device.

v0:
```python
import jax
import jax.numpy as jnp
from jax import lax
from jax.sharding import PartitionSpec as P


def passed_along(array, axis, by):
    count = lax.axis_size(axis)
    return lax.ppermute(array, axis, [(i, (i + by) % count) for i in range(count)])


def left_apply(matrix, vector):
    return lax.dot_general(
        matrix,
        vector,
        (((1,), (0,)), ((), ())),
        precision=lax.Precision.HIGHEST,
        preferred_element_type=jnp.float32,
    )


def right_apply(vector, matrix):
    return jnp.dot(
        vector, matrix, precision=lax.Precision.HIGHEST, preferred_element_type=jnp.float32
    )


def apply_dual(window, basis, couplings, live):
    projected = left_apply(basis, window)
    inner = projected
    summed = jnp.zeros_like(window)
    for slot, coupling in enumerate(couplings):
        distance = slot + 1
        ahead = passed_along(window, "col", -distance)
        inner = inner + live[slot] * left_apply(coupling, ahead)
        back = live[slot] * right_apply(projected, coupling)
        summed = summed + passed_along(back, "col", distance)
    return summed + right_apply(inner, basis)


def on_device(sub_basis, coupling, pair_live, offsets, dual_in):
    width = sub_basis.shape[2]
    basis = sub_basis[0].astype(jnp.float32)
    couplings = [coupling[0, h].astype(jnp.float32) for h in range(coupling.shape[1])]
    live = pair_live[0].astype(jnp.float32)
    length = dual_in.shape[1] * lax.axis_size("row")
    start = offsets[0]
    piece = dual_in
    for _ in range(2):
        column = lax.all_gather(piece, "row", axis=1, tiled=True)[0]
        window = lax.dynamic_slice_in_dim(column, start, width)
        local = apply_dual(window, basis, couplings, live)
        placed = lax.dynamic_update_slice(jnp.zeros((length,), jnp.float32), local, (start,))
        piece = lax.psum_scatter(placed[None, :], "row", scatter_dimension=1, tiled=True)
    return piece


def solution(mesh):
    return jax.shard_map(
        on_device,
        mesh=mesh,
        in_specs=(
            P(("row", "col"), None, None),
            P(("row", "col"), None, None, None),
            P(("row", "col"), None),
            P(("row", "col")),
            P("col", "row"),
        ),
        out_specs=P("col", "row"),
        check_vma=False,
    )
```

profile of v0, /device:TPU:0, one launch (start us, length us, event | category | flops | bytes accessed | tf_op | source)
XLA Modules:
  0.0 154.4 jit_solution(13610832899957684372)
XLA Ops:
  7.3 10.5 %all_gather.6 = f32[1,4096]{1,0:T(1,128)S(1)} all-gather(f32[1,512]{1,0:T(1,128)} %param.9), channel_id=1, replica_groups=mesh['row'=8,'col'=4] {'row'}, dimensions={1}, use_global_device_ids=true | all-gather | bytes 18432 | tf_op jit(solution)/shard_map/all_gather | solution.py:50
  17.8 0.1 dynamic-slice_reduce_fusion.1
  17.9 0.0 copy-start.1
  17.9 3.7 %collective-permute-start.2 = (f32[768]{0:T(1024)S(1)}, f32[768]{0:T(1024)S(1)}, u32[]{:S(2)}, u32[]{:S(2)}) collective-permute-start(f32[768]{0:T(1024)S(1)} %dynamic-slice_reduce_fusion.1), channel_id=1, source_target_pairs={{0,3},{1,0},{2,1},{3,2},{4,7},{5,4},{6,5},{7,6},{8,11},{9,8},{10,9... | collective-permute-start | bytes 9224 | tf_op jit(solution)/shard_map/ppermute | solution.py:9
  21.5 0.0 collective-permute-start.3
  21.5 1.1 fusion.73
  22.7 0.6 fusion.72
  23.2 1.9 %fusion.30 = f32[768]{0:T(1024)S(1)} fusion(bf16[1,2,768,768]{3,2,1,0:T(8,128)(2,1)} %param.6, f32[1,768]{1,0:T(1,128)S(1)} %get-tuple-element.8), kind=kOutput, calls=%fused_computation.26 | convolution fusion | flops 7077888 | bytes 1185792 | tf_op jit(solution)/shard_map/dot_general | solution.py:23
  25.1 0.7 broadcast_multiply_fusion.3
  25.8 1.1 collective-permute-start
  26.8 0.6 fusion.42
  27.4 0.6 broadcast_multiply_fusion.1
  28.0 2.0 %collective-permute-start.1 = (f32[768]{0:T(1024)S(1)}, f32[768]{0:T(1024)S(1)}, u32[]{:S(2)}, u32[]{:S(2)}) collective-permute-start(f32[768]{0:T(1024)S(1)} %broadcast_multiply_fusion.1), channel_id=1, source_target_pairs={{0,2},{1,3},{2,0},{3,1},{4,6},{5,7},{6,4},{7,5},{8,10},{9,11},{10,... | collective-permute-start | bytes 9224 | tf_op jit(solution)/shard_map/ppermute | solution.py:9
  30.0 0.0 collective-permute-done.2
  30.0 1.1 fusion.33
  31.1 0.0 collective-permute-done.3
  31.1 1.1 fusion.45
  32.2 1.2 multiply_add_fusion.1
  33.4 0.6 fusion.24
  34.0 0.0 collective-permute-done
  34.0 0.0 collective-permute-done.1
  34.0 0.6 broadcast_in_dim.9
  34.6 0.8 dynamic_update_slice.8
  35.5 2.0 %copy.6 = f32[1,4096]{0,1:T(8,128)} copy(f32[1,4096]{1,0:T(1,128)S(1)} %dynamic_update_slice.8) | data formatting | bytes 32768
  37.5 0.0 reduce-scatter.7.cloned.1.call-update
  37.5 0.0 reduce-scatter.9.cloned.1.call-start
  37.5 41.0 %reduce-scatter.7.cloned.1.call-done = f32[512,1]{1,0:T(8,128)} async-done(((f32[4096,1]{1,0:T(8,128)}), f32[512,1]{1,0:T(8,128)}) %reduce-scatter.7.cloned.1.call-update) | async-done | bytes 2064
  78.6 1.1 copy.7
  79.6 8.8 %all_gather.7 = f32[1,4096]{1,0:T(1,128)S(1)} all-gather(f32[1,512]{1,0:T(1,128)S(1)} %copy.7), channel_id=1, replica_groups=mesh['row'=8,'col'=4] {'row'}, dimensions={1}, use_global_device_ids=true | all-gather | bytes 18432 | tf_op jit(solution)/shard_map/all_gather | solution.py:50
  88.5 0.1 dynamic-slice_reduce_fusion
  88.6 3.4 %collective-permute-start.6 = (f32[768]{0:T(1024)S(1)}, f32[768]{0:T(1024)S(1)}, u32[]{:S(2)}, u32[]{:S(2)}) collective-permute-start(f32[768]{0:T(1024)S(1)} %dynamic-slice_reduce_fusion), channel_id=1, source_target_pairs={{0,3},{1,0},{2,1},{3,2},{4,7},{5,4},{6,5},{7,6},{8,11},{9,8},{10,9... | collective-permute-start | bytes 9224 | tf_op jit(solution)/shard_map/ppermute | solution.py:9
  91.9 0.0 collective-permute-start.7
  91.9 1.1 fusion.74
  93.0 0.6 fusion.36
  93.6 0.6 fusion.48
  94.2 0.7 broadcast_multiply_fusion.2
  94.9 1.1 collective-permute-start.4
  96.0 0.6 broadcast_multiply_fusion
  96.6 1.9 %collective-permute-start.5 = (f32[768]{0:T(1024)S(1)}, f32[768]{0:T(1024)S(1)}, u32[]{:S(2)}, u32[]{:S(2)}) collective-permute-start(f32[768]{0:T(1024)S(1)} %broadcast_multiply_fusion), channel_id=1, source_target_pairs={{0,2},{1,3},{2,0},{3,1},{4,6},{5,7},{6,4},{7,5},{8,10},{9,11},{10,... | collective-permute-start | bytes 9224 | tf_op jit(solution)/shard_map/ppermute | solution.py:9
  98.5 1.1 fusion.39
  99.6 1.1 fusion.51
  100.7 1.2 multiply_add_fusion
  101.9 0.6 fusion.27
  102.6 0.2 dynamic_update_slice.9
  102.8 2.0 %copy.8 = f32[1,4096]{0,1:T(8,128)} copy(f32[1,4096]{1,0:T(1,128)S(1)} %dynamic_update_slice.9) | data formatting | bytes 32768
  104.8 0.0 reduce-scatter.9.cloned.1.call-update
  104.8 41.1 %reduce-scatter.9.cloned.1.call-done = f32[512,1]{1,0:T(8,128)} async-done(((f32[4096,1]{1,0:T(8,128)}), f32[512,1]{1,0:T(8,128)}) %reduce-scatter.9.cloned.1.call-update) | async-done | bytes 2064
  145.9 1.6 %copy.9 = f32[1,512]{1,0:T(1,128)} copy(f32[1,512]{0,1:T(8,128)} %bitcast.90) | data formatting | bytes 4096
  (22 shorter events, 0.1 us)
Async XLA Ops:
  6.5 15.0 %copy-start = (bf16[1,768,768]{2,1,0:T(8,128)(2,1)S(1)}, bf16[1,768,768]{2,1,0:T(8,128)(2,1)}, u32[]{:S(2)}) copy-start(bf16[1,768,768]{2,1,0:T(8,128)(2,1)} %param.5) | copy-start | bytes 3538948
  6.5 72.0 %reduce-scatter.7.cloned.1.call-start = ((), (), s32[]{:S(2)}) async-start(), calls=%async_computation.2 | async-start | bytes 2359296
  17.8 4.9 %copy-start.2 = (s32[1,2]{1,0:T(1,128)S(1)}, s32[1,2]{1,0:T(1,128)}, u32[]{:S(2)}) copy-start(s32[1,2]{1,0:T(1,128)} %param.7) | copy-start | bytes 28
  17.9 9.0 %copy-start.1 = (bf16[1,2,768,768]{3,2,1,0:T(8,128)(2,1)S(1)}, bf16[1,2,768,768]{3,2,1,0:T(8,128)(2,1)}, u32[]{:S(2)}) copy-start(bf16[1,2,768,768]{3,2,1,0:T(8,128)(2,1)} %param.6) | copy-start | bytes 7077892
  17.9 12.1 %collective-permute-start.2 = (f32[768]{0:T(1024)S(1)}, f32[768]{0:T(1024)S(1)}, u32[]{:S(2)}, u32[]{:S(2)}) collective-permute-start(f32[768]{0:T(1024)S(1)} %dynamic-slice_reduce_fusion.1), channel_id=1, source_target_pairs={{0,3},{1,0},{2,1},{3,2},{4,7},{5,4},{6,5},{7,6},{8,11},{9,8},{10,9... | collective-permute-start | bytes 9224 | tf_op jit(solution)/shard_map/ppermute | solution.py:9
  21.5 9.5 %collective-permute-start.3 = (f32[768]{0:T(1024)S(1)}, f32[768]{0:T(1024)S(1)}, u32[]{:S(2)}, u32[]{:S(2)}) collective-permute-start(f32[768]{0:T(1024)S(1)} %dynamic-slice_reduce_fusion.1), channel_id=1, source_target_pairs={{0,2},{1,3},{2,0},{3,1},{4,6},{5,7},{6,4},{7,5},{8,10},{9,11},{10,... | collective-permute-start | bytes 9224 | tf_op jit(solution)/shard_map/ppermute | solution.py:9
  25.8 8.2 %collective-permute-start = (f32[768]{0:T(1024)S(1)}, f32[768]{0:T(1024)S(1)}, u32[]{:S(2)}, u32[]{:S(2)}) collective-permute-start(f32[768]{0:T(1024)S(1)} %broadcast_multiply_fusion.3), channel_id=1, source_target_pairs={{0,1},{1,2},{2,3},{3,0},{4,5},{5,6},{6,7},{7,4},{8,9},{9,10},{10,1... | collective-permute-start | bytes 9224 | tf_op jit(solution)/shard_map/ppermute | solution.py:9
  28.0 6.0 %collective-permute-start.1 = (f32[768]{0:T(1024)S(1)}, f32[768]{0:T(1024)S(1)}, u32[]{:S(2)}, u32[]{:S(2)}) collective-permute-start(f32[768]{0:T(1024)S(1)} %broadcast_multiply_fusion.1), channel_id=1, source_target_pairs={{0,2},{1,3},{2,0},{3,1},{4,6},{5,7},{6,4},{7,5},{8,10},{9,11},{10,... | collective-permute-start | bytes 9224 | tf_op jit(solution)/shard_map/ppermute | solution.py:9
  37.5 108.4 %reduce-scatter.9.cloned.1.call-start = ((), (), s32[]{:S(2)}) async-start(), calls=%async_computation.3 | async-start | bytes 2359296
  88.6 10.0 %collective-permute-start.6 = (f32[768]{0:T(1024)S(1)}, f32[768]{0:T(1024)S(1)}, u32[]{:S(2)}, u32[]{:S(2)}) collective-permute-start(f32[768]{0:T(1024)S(1)} %dynamic-slice_reduce_fusion), channel_id=1, source_target_pairs={{0,3},{1,0},{2,1},{3,2},{4,7},{5,4},{6,5},{7,6},{8,11},{9,8},{10,9... | collective-permute-start | bytes 9224 | tf_op jit(solution)/shard_map/ppermute | solution.py:9
  91.9 7.7 %collective-permute-start.7 = (f32[768]{0:T(1024)S(1)}, f32[768]{0:T(1024)S(1)}, u32[]{:S(2)}, u32[]{:S(2)}) collective-permute-start(f32[768]{0:T(1024)S(1)} %dynamic-slice_reduce_fusion), channel_id=1, source_target_pairs={{0,2},{1,3},{2,0},{3,1},{4,6},{5,7},{6,4},{7,5},{8,10},{9,11},{10,... | collective-permute-start | bytes 9224 | tf_op jit(solution)/shard_map/ppermute | solution.py:9
  94.9 7.6 %collective-permute-start.4 = (f32[768]{0:T(1024)S(1)}, f32[768]{0:T(1024)S(1)}, u32[]{:S(2)}, u32[]{:S(2)}) collective-permute-start(f32[768]{0:T(1024)S(1)} %broadcast_multiply_fusion.2), channel_id=1, source_target_pairs={{0,1},{1,2},{2,3},{3,0},{4,5},{5,6},{6,7},{7,4},{8,9},{9,10},{10,1... | collective-permute-start | bytes 9224 | tf_op jit(solution)/shard_map/ppermute | solution.py:9
  96.6 5.9 %collective-permute-start.5 = (f32[768]{0:T(1024)S(1)}, f32[768]{0:T(1024)S(1)}, u32[]{:S(2)}, u32[]{:S(2)}) collective-permute-start(f32[768]{0:T(1024)S(1)} %broadcast_multiply_fusion), channel_id=1, source_target_pairs={{0,2},{1,3},{2,0},{3,1},{4,6},{5,7},{6,4},{7,5},{8,10},{9,11},{10,... | collective-permute-start | bytes 9224 | tf_op jit(solution)/shard_map/ppermute | solution.py:9
Sparse Core Ops, SparseCore 0:
  37.6 40.9 reduce-scatter.6
  104.9 40.9 reduce-scatter.8
where the time goes:
time: 155 us; the launch traced here: 154 us
  waiting for transfers between devices  82.2 us (53%)
  blocking collectives  19.3 us (12%)
  between operations  14.5 us (9%)
  starting transfers between devices  13.2 us (9%)
  matrix products  11.3 us (7%)
  local copies, waits for them, and re-layouts  9.11 us (6%)
  other arithmetic  4.85 us (3%)
    unnamed x4, waiting for transfers between devices  82.2 us
    all_gather x2, blocking collectives, on_device(): column = lax.all_gather(piece, 'row', axis=1, tiled=True)[0]  19.3 us
    ppermute x8, starting transfers between devices, passed_along(): lax.ppermute(array, axis, [(i, (i + by) % count) for i in range(count)])  13.1 us
    unnamed x10, local copies, waits for them, and re-layouts  6.72 us
    dot_general x6, matrix products, left_apply(): lax.dot_general(matrix, vector, (((1,), (0,)), ((), ())), precision=lax.P...  6.42 us
    dot_general x6, matrix products, right_apply(): jnp.dot(vector, matrix, precision=lax.Precision.HIGHEST, preferred_elemen...  4.84 us
  transfers between devices with their start and end apart: 10, of which 2 were waited for; matrix products, arithmetic and copies ran while one was open for 11% of the time, Pallas kernels for 0%

commit v1 on v0

--- a/solution.py
+++ b/solution.py
@@ -1,7 +1,26 @@
+import functools
 import jax
 import jax.numpy as jnp
 from jax import lax
 from jax.sharding import PartitionSpec as P
+
+
+def see_clusters(piece_in, axis_id):
+    reply, arr_now = (lax.psum(1, axis_id), lax.axis_index(axis_id))
+    t1, block_next = (piece_in, 1)
+    while block_next < reply:
+        xs_all = []
+        for b in range(reply):
+            xs_all.append((b, b ^ block_next))
+        now = lax.ppermute(t1, axis_id, xs_all)
+        piece_now = jnp.concatenate([t1, now], 1)
+        reached = jnp.concatenate([now, t1], 1)
+        t1 = jnp.where(arr_now & block_next == 0, piece_now, reached)
+        block_next = 2 * block_next
+    return t1
+
+
+scan_gates = functools.partial(see_clusters, axis_id="row")
 
 
 def passed_along(array, axis, by):
@@ -47,7 +66,7 @@
     start = offsets[0]
     piece = dual_in
     for _ in range(2):
-        column = lax.all_gather(piece, "row", axis=1, tiled=True)[0]
+        column = scan_gates(piece)[0]
         window = lax.dynamic_slice_in_dim(column, start, width)
         local = apply_dual(window, basis, couplings, live)
         placed = lax.dynamic_update_slice(jnp.zeros((length,), jnp.float32), local, (start,))

time: 155 us -> 155 us (level)
  blocking collectives: 19.3 us -> 0 us
  waiting for transfers between devices: 82.2 us -> 91.2 us
  starting transfers between devices: 13.2 us -> 21.8 us
  other arithmetic: 4.85 us -> 7.2 us
    all_gather x2 -> x0, blocking collectives: 19.3 us -> none  [on_device(): column = lax.all_gather(piece, 'row', axis=1, tiled=True)[0]]
    ppermute x0 -> x6, starting transfers between devices: none -> 8.13 us  [see_clusters(): now = lax.ppermute(t1, axis_id, xs_all)]
    ppermute x0 -> x6, waiting for transfers between devices: none -> 7.97 us  [see_clusters(): now = lax.ppermute(t1, axis_id, xs_all)]
    select_n x0 -> x8, other arithmetic: none -> 1.57 us  [see_clusters(): t1 = jnp.where(arr_now & block_next == 0, piece_now, reached)]
    unnamed x10 -> x8, local copies, waits for them, and re-layouts: 6.72 us -> 6.71 us
  transfers between devices with their start and end apart: 10 -> 16, of which waited for: 2 -> 7; matrix products, arithmetic and copies ran while one was open for 11% -> 12% of each run, Pallas kernels for 0% -> 0%
where the time goes in v1:
time: 155 us
  waiting for transfers between devices  91.2 us (59%)
  starting transfers between devices  21.8 us (14%)
  between operations  14.4 us (9%)
  matrix products  11.2 us (7%)
  local copies, waits for them, and re-layouts  8.94 us (6%)
  other arithmetic  7.2 us (5%)
    unnamed x4, waiting for transfers between devices  83.2 us
    ppermute x8, starting transfers between devices, passed_along(): lax.ppermute(array, axis, [(i, (i + by) % count) for i in range(count)])  13.6 us
    ppermute x6, starting transfers between devices, see_clusters(): now = lax.ppermute(t1, axis_id, xs_all)  8.13 us
    ppermute x6, waiting for transfers between devices, see_clusters(): now = lax.ppermute(t1, axis_id, xs_all)  7.97 us
    unnamed x8, local copies, waits for them, and re-layouts  6.71 us
    dot_general x6, matrix products, left_apply(): lax.dot_general(matrix, vector, (((1,), (0,)), ((), ())), precision=lax.P...  6.39 us
    dot_general x6, matrix products, right_apply(): jnp.dot(vector, matrix, precision=lax.Precision.HIGHEST, preferred_elemen...  4.85 us
  transfers between devices with their start and end apart: 16, of which 7 were waited for; matrix products, arithmetic and copies ran while one was open for 12% of the time, Pallas kernels for 0%

profile of v1, /device:TPU:0, one launch (start us, length us, event | category | flops | bytes accessed | tf_op | source)
XLA Modules:
  0.0 154.7 jit_solution(4331321858795208120)
XLA Ops:
  6.5 0.5 collective-permute-start
  7.0 0.7 convert_element_type.3
  7.7 0.6 fusion.74
  8.9 0.8 broadcast_select_fusion.3
  9.7 2.6 %collective-permute-start.1 = (f32[1,1024]{1,0:T(1,128)S(1)}, f32[1,1024]{1,0:T(1,128)S(1)}, u32[]{:S(2)}, u32[]{:S(2)}) collective-permute-start(f32[1,1024]{1,0:T(1,128)S(1)} %broadcast_select_fusion.3), channel_id=1, source_target_pairs={{0,8},{4,12},{8,0},{12,4},{16,24},{20,28},{24,16},{28,20},{1,9},{5... | collective-permute-start | bytes 12296 | tf_op jit(solution)/shard_map/ppermute | solution.py:15
  12.3 0.8 maximum_select_fusion.2
  13.0 0.8 collective-permute-done.1
  13.9 2.1 %collective-permute-start.2 = (f32[1,2048]{1,0:T(1,128)S(1)}, f32[1,2048]{1,0:T(1,128)S(1)}, u32[]{:S(2)}, u32[]{:S(2)}) collective-permute-start(f32[1,2048]{1,0:T(1,128)S(1)} %broadcast_select_fusion.1), channel_id=1, source_target_pairs={{0,16},{4,20},{8,24},{12,28},{16,0},{20,4},{24,8},{28,12},{1,17},{... | collective-permute-start | bytes 24584 | tf_op jit(solution)/shard_map/ppermute | solution.py:15
  16.0 1.6 %collective-permute-done.2 = f32[1,2048]{1,0:T(1,128)S(1)} collective-permute-done((f32[1,2048]{1,0:T(1,128)S(1)}, f32[1,2048]{1,0:T(1,128)S(1)}, u32[]{:S(2)}, u32[]{:S(2)}) %collective-permute-start.2) | collective-permute-done | bytes 8224 | tf_op jit(solution)/shard_map/ppermute | solution.py:15
  17.7 4.2 %collective-permute-start.5 = (f32[768]{0:T(1024)S(1)}, f32[768]{0:T(1024)S(1)}, u32[]{:S(2)}, u32[]{:S(2)}) collective-permute-start(f32[768]{0:T(1024)S(1)} %get-tuple-element.7), channel_id=1, source_target_pairs={{0,3},{1,0},{2,1},{3,2},{4,7},{5,4},{6,5},{7,6},{8,11},{9,8},{10,9... | collective-permute-start | bytes 9224 | tf_op jit(solution)/shard_map/ppermute | solution.py:28
  21.9 1.1 fusion.75
  23.0 1.9 %fusion.30 = f32[768]{0:T(1024)S(1)} fusion(bf16[1,2,768,768]{3,2,1,0:T(8,128)(2,1)} %param.6, f32[1,768]{1,0:T(1,128)S(1)} %get-tuple-element.12), kind=kOutput, calls=%fused_computation.26 | convolution fusion | flops 7077888 | bytes 1185792 | tf_op jit(solution)/shard_map/dot_general | solution.py:42
  24.8 0.6 fusion.42
  25.4 0.6 broadcast_multiply_fusion.3
  26.0 1.1 collective-permute-start.3
  27.1 0.6 broadcast_multiply_fusion.1
  27.7 2.0 %collective-permute-start.4 = (f32[768]{0:T(1024)S(1)}, f32[768]{0:T(1024)S(1)}, u32[]{:S(2)}, u32[]{:S(2)}) collective-permute-start(f32[768]{0:T(1024)S(1)} %broadcast_multiply_fusion.1), channel_id=1, source_target_pairs={{0,2},{1,3},{2,0},{3,1},{4,6},{5,7},{6,4},{7,5},{8,10},{9,11},{10,... | collective-permute-start | bytes 9224 | tf_op jit(solution)/shard_map/ppermute | solution.py:28
  29.7 1.1 fusion.33
  30.8 1.1 fusion.45
  31.9 1.2 multiply_add_fusion.1
  33.1 0.6 fusion.24
  33.7 0.6 broadcast_in_dim.9
  34.3 0.8 dynamic_update_slice.8
  35.2 2.0 %copy.6 = f32[1,4096]{0,1:T(8,128)} copy(f32[1,4096]{1,0:T(1,128)S(1)} %dynamic_update_slice.8) | data formatting | bytes 32768
  37.2 42.0 %reduce-scatter.7.cloned.1.call-done = f32[512,1]{1,0:T(8,128)} async-done(((f32[4096,1]{1,0:T(8,128)}), f32[512,1]{1,0:T(8,128)}) %reduce-scatter.7.cloned.1.call-update) | async-done | bytes 2064
  79.2 1.1 copy.7
  80.4 1.1 collective-permute-done.7
  81.5 1.4 collective-permute-start.8
  82.9 2.2 %collective-permute-done.8 = f32[1,1024]{1,0:T(1,128)S(1)} collective-permute-done((f32[1,1024]{1,0:T(1,128)S(1)}, f32[1,1024]{1,0:T(1,128)S(1)}, u32[]{:S(2)}, u32[]{:S(2)}) %collective-permute-start.8) | collective-permute-done | bytes 4128 | tf_op jit(solution)/shard_map/ppermute | solution.py:15
  85.1 1.5 collective-permute-start.9
  86.6 2.2 %collective-permute-done.9 = f32[1,2048]{1,0:T(1,128)S(1)} collective-permute-done((f32[1,2048]{1,0:T(1,128)S(1)}, f32[1,2048]{1,0:T(1,128)S(1)}, u32[]{:S(2)}, u32[]{:S(2)}) %collective-permute-start.9) | collective-permute-done | bytes 8224 | tf_op jit(solution)/shard_map/ppermute | solution.py:15
  88.8 0.1 fusion.72
  89.0 3.4 %collective-permute-start.12 = (f32[768]{0:T(1024)S(1)}, f32[768]{0:T(1024)S(1)}, u32[]{:S(2)}, u32[]{:S(2)}) collective-permute-start(f32[768]{0:T(1024)S(1)} %get-tuple-element.5), channel_id=1, source_target_pairs={{0,3},{1,0},{2,1},{3,2},{4,7},{5,4},{6,5},{7,6},{8,11},{9,8},{10,9... | collective-permute-start | bytes 9224 | tf_op jit(solution)/shard_map/ppermute | solution.py:28
  92.3 1.1 fusion.76
  93.4 0.6 fusion.36
  94.0 0.6 fusion.48
  94.6 0.6 broadcast_multiply_fusion.2
  95.2 1.1 collective-permute-start.10
  96.3 0.6 broadcast_multiply_fusion
  97.0 1.9 %collective-permute-start.11 = (f32[768]{0:T(1024)S(1)}, f32[768]{0:T(1024)S(1)}, u32[]{:S(2)}, u32[]{:S(2)}) collective-permute-start(f32[768]{0:T(1024)S(1)} %broadcast_multiply_fusion), channel_id=1, source_target_pairs={{0,2},{1,3},{2,0},{3,1},{4,6},{5,7},{6,4},{7,5},{8,10},{9,11},{10,... | collective-permute-start | bytes 9224 | tf_op jit(solution)/shard_map/ppermute | solution.py:28
  98.9 1.1 fusion.39
  100.0 1.1 fusion.51
  101.1 1.2 multiply_add_fusion
  102.3 0.6 fusion.27
  102.9 0.2 dynamic_update_slice.9
  103.1 2.0 %copy.8 = f32[1,4096]{0,1:T(8,128)} copy(f32[1,4096]{1,0:T(1,128)S(1)} %dynamic_update_slice.9) | data formatting | bytes 32768
  105.1 41.1 %reduce-scatter.9.cloned.1.call-done = f32[512,1]{1,0:T(8,128)} async-done(((f32[4096,1]{1,0:T(8,128)}), f32[512,1]{1,0:T(8,128)}) %reduce-scatter.9.cloned.1.call-update) | async-done | bytes 2064
  146.3 1.6 %copy.9 = f32[1,512]{1,0:T(1,128)} copy(f32[1,512]{0,1:T(8,128)} %bitcast.100) | data formatting | bytes 4096
  (38 shorter events, 0.4 us)
Async XLA Ops:
  6.5 15.4 %copy-start = (bf16[1,768,768]{2,1,0:T(8,128)(2,1)S(1)}, bf16[1,768,768]{2,1,0:T(8,128)(2,1)}, u32[]{:S(2)}) copy-start(bf16[1,768,768]{2,1,0:T(8,128)(2,1)} %param.5) | copy-start | bytes 3538948
  6.5 72.7 %reduce-scatter.7.cloned.1.call-start = ((), (), s32[]{:S(2)}) async-start(), calls=%async_computation.2 | async-start | bytes 2359296
  6.5 2.4 %collective-permute-start = (f32[1,512]{1,0:T(1,128)}, f32[1,512]{1,0:T(1,128)S(1)}, u32[]{:S(2)}, u32[]{:S(2)}) collective-permute-start(f32[1,512]{1,0:T(1,128)} %param.9), channel_id=1, source_target_pairs={{0,4},{4,0},{8,12},{12,8},{16,20},{20,16},{24,28},{28,24},{1,5},{5... | collective-permute-start | bytes 6152 | tf_op jit(solution)/shard_map/ppermute | solution.py:15
  9.7 4.2 %collective-permute-start.1 = (f32[1,1024]{1,0:T(1,128)S(1)}, f32[1,1024]{1,0:T(1,128)S(1)}, u32[]{:S(2)}, u32[]{:S(2)}) collective-permute-start(f32[1,1024]{1,0:T(1,128)S(1)} %broadcast_select_fusion.3), channel_id=1, source_target_pairs={{0,8},{4,12},{8,0},{12,4},{16,24},{20,28},{24,16},{28,20},{1,9},{5... | collective-permute-start | bytes 12296 | tf_op jit(solution)/shard_map/ppermute | solution.py:15
  13.9 3.7 %collective-permute-start.2 = (f32[1,2048]{1,0:T(1,128)S(1)}, f32[1,2048]{1,0:T(1,128)S(1)}, u32[]{:S(2)}, u32[]{:S(2)}) collective-permute-start(f32[1,2048]{1,0:T(1,128)S(1)} %broadcast_select_fusion.1), channel_id=1, source_target_pairs={{0,16},{4,20},{8,24},{12,28},{16,0},{20,4},{24,8},{28,12},{1,17},{... | collective-permute-start | bytes 24584 | tf_op jit(solution)/shard_map/ppermute | solution.py:15
  17.7 12.0 %collective-permute-start.5 = (f32[768]{0:T(1024)S(1)}, f32[768]{0:T(1024)S(1)}, u32[]{:S(2)}, u32[]{:S(2)}) collective-permute-start(f32[768]{0:T(1024)S(1)} %get-tuple-element.7), channel_id=1, source_target_pairs={{0,3},{1,0},{2,1},{3,2},{4,7},{5,4},{6,5},{7,6},{8,11},{9,8},{10,9... | collective-permute-start | bytes 9224 | tf_op jit(solution)/shard_map/ppermute | solution.py:28
  21.9 8.9 %collective-permute-start.6 = (f32[768]{0:T(1024)S(1)}, f32[768]{0:T(1024)S(1)}, u32[]{:S(2)}, u32[]{:S(2)}) collective-permute-start(f32[768]{0:T(1024)S(1)} %get-tuple-element.7), channel_id=1, source_target_pairs={{0,2},{1,3},{2,0},{3,1},{4,6},{5,7},{6,4},{7,5},{8,10},{9,11},{10,... | collective-permute-start | bytes 9224 | tf_op jit(solution)/shard_map/ppermute | solution.py:28
  21.9 3.0 %copy-start.1 = (bf16[1,2,768,768]{3,2,1,0:T(8,128)(2,1)S(1)}, bf16[1,2,768,768]{3,2,1,0:T(8,128)(2,1)}, u32[]{:S(2)}) copy-start(bf16[1,2,768,768]{3,2,1,0:T(8,128)(2,1)} %param.6) | copy-start | bytes 7077892
  26.0 7.7 %collective-permute-start.3 = (f32[768]{0:T(1024)S(1)}, f32[768]{0:T(1024)S(1)}, u32[]{:S(2)}, u32[]{:S(2)}) collective-permute-start(f32[768]{0:T(1024)S(1)} %broadcast_multiply_fusion.3), channel_id=1, source_target_pairs={{0,1},{1,2},{2,3},{3,0},{4,5},{5,6},{6,7},{7,4},{8,9},{9,10},{10,1... | collective-permute-start | bytes 9224 | tf_op jit(solution)/shard_map/ppermute | solution.py:28
  27.7 6.0 %collective-permute-start.4 = (f32[768]{0:T(1024)S(1)}, f32[768]{0:T(1024)S(1)}, u32[]{:S(2)}, u32[]{:S(2)}) collective-permute-start(f32[768]{0:T(1024)S(1)} %broadcast_multiply_fusion.1), channel_id=1, source_target_pairs={{0,2},{1,3},{2,0},{3,1},{4,6},{5,7},{6,4},{7,5},{8,10},{9,11},{10,... | collective-permute-start | bytes 9224 | tf_op jit(solution)/shard_map/ppermute | solution.py:28
  37.2 109.1 %reduce-scatter.9.cloned.1.call-start = ((), (), s32[]{:S(2)}) async-start(), calls=%async_computation.3 | async-start | bytes 2359296
  80.3 1.2 collective-permute-start.7
  81.5 3.6 %collective-permute-start.8 = (f32[1,1024]{1,0:T(1,128)S(1)}, f32[1,1024]{1,0:T(1,128)S(1)}, u32[]{:S(2)}, u32[]{:S(2)}) collective-permute-start(f32[1,1024]{1,0:T(1,128)S(1)} %broadcast_select_fusion.2), channel_id=1, source_target_pairs={{0,8},{4,12},{8,0},{12,4},{16,24},{20,28},{24,16},{28,20},{1,9},{5... | collective-permute-start | bytes 12296 | tf_op jit(solution)/shard_map/ppermute | solution.py:15
  85.1 3.7 %collective-permute-start.9 = (f32[1,2048]{1,0:T(1,128)S(1)}, f32[1,2048]{1,0:T(1,128)S(1)}, u32[]{:S(2)}, u32[]{:S(2)}) collective-permute-start(f32[1,2048]{1,0:T(1,128)S(1)} %broadcast_select_fusion), channel_id=1, source_target_pairs={{0,16},{4,20},{8,24},{12,28},{16,0},{20,4},{24,8},{28,12},{1,17},{... | collective-permute-start | bytes 24584 | tf_op jit(solution)/shard_map/ppermute | solution.py:15
  89.0 9.9 %collective-permute-start.12 = (f32[768]{0:T(1024)S(1)}, f32[768]{0:T(1024)S(1)}, u32[]{:S(2)}, u32[]{:S(2)}) collective-permute-start(f32[768]{0:T(1024)S(1)} %get-tuple-element.5), channel_id=1, source_target_pairs={{0,3},{1,0},{2,1},{3,2},{4,7},{5,4},{6,5},{7,6},{8,11},{9,8},{10,9... | collective-permute-start | bytes 9224 | tf_op jit(solution)/shard_map/ppermute | solution.py:28
  92.3 7.6 %collective-permute-start.13 = (f32[768]{0:T(1024)S(1)}, f32[768]{0:T(1024)S(1)}, u32[]{:S(2)}, u32[]{:S(2)}) collective-permute-start(f32[768]{0:T(1024)S(1)} %get-tuple-element.5), channel_id=1, source_target_pairs={{0,2},{1,3},{2,0},{3,1},{4,6},{5,7},{6,4},{7,5},{8,10},{9,11},{10,... | collective-permute-start | bytes 9224 | tf_op jit(solution)/shard_map/ppermute | solution.py:28
  95.2 7.7 %collective-permute-start.10 = (f32[768]{0:T(1024)S(1)}, f32[768]{0:T(1024)S(1)}, u32[]{:S(2)}, u32[]{:S(2)}) collective-permute-start(f32[768]{0:T(1024)S(1)} %broadcast_multiply_fusion.2), channel_id=1, source_target_pairs={{0,1},{1,2},{2,3},{3,0},{4,5},{5,6},{6,7},{7,4},{8,9},{9,10},{10,1... | collective-permute-start | bytes 9224 | tf_op jit(solution)/shard_map/ppermute | solution.py:28
  97.0 5.9 %collective-permute-start.11 = (f32[768]{0:T(1024)S(1)}, f32[768]{0:T(1024)S(1)}, u32[]{:S(2)}, u32[]{:S(2)}) collective-permute-start(f32[768]{0:T(1024)S(1)} %broadcast_multiply_fusion), channel_id=1, source_target_pairs={{0,2},{1,3},{2,0},{3,1},{4,6},{5,7},{6,4},{7,5},{8,10},{9,11},{10,... | collective-permute-start | bytes 9224 | tf_op jit(solution)/shard_map/ppermute | solution.py:28
Sparse Core Ops, SparseCore 0:
  37.3 41.8 reduce-scatter.6
  105.3 40.9 reduce-scatter.8
